TPU v7x, 32 devices: a whole 2x2x4 slice. The times are simulated.
32 devices in a mesh: pages: 2 (over y), tile: 8 (over z, x), mp: 2 (over core).
Axes of the slice: x: 2, y: 2, z: 4, core: 2. Of those that a mesh axis runs over, the one named last changes fastest.
Arguments:
- queries: bfloat16 [3072, 1024], P(('pages', 'tile'), 'mp'), parts along dimension 0, may hold values from -10.5 to 10.5
- key_rows: bfloat16 [3072, 1024], P(('pages', 'tile'), 'mp'), parts along dimension 0, may hold values from -8.5 to 8.5
- value_rows: bfloat16 [3072, 1024], P(('pages', 'tile'), 'mp'), parts along dimension 0, may hold values from -6 to 6
- grad_out: bfloat16 [3072, 1024], P(('pages', 'tile'), 'mp'), parts along dimension 0, may hold values from -6 to 6
- owner_shard: int32 [3072], P(('pages', 'tile')), parts along dimension 0, may hold values from 0 to 7, as said below
- logit_scale: float32 [16], P('mp'), may hold values from 0.5 to 2
Outputs:
- grad_queries: bfloat16 [3072, 1024], P(('pages', 'tile'), 'mp'), parts along dimension 0
- grad_keys: bfloat16 [3072, 1024], P(('pages', 'tile'), 'mp'), parts along dimension 0
- grad_values: bfloat16 [3072, 1024], P(('pages', 'tile'), 'mp'), parts along dimension 0
There are 2 independent parts, one for each index of `pages`. A program takes and returns all parts, laid end to end along the dimension named above; an argument that names none is the same for every part. Nothing has to cross between parts.
Inputs may be any that keep to these rules, and one draw needn't show every extreme that they name: `owner_shard`: the 192 tokens of one index of tile name any one region at most 48 times; in every draw one region is named exactly 48 times by the tokens of every index of tile, so it holds 384 tokens.
All inputs are finite; a program needn't handle non-finite values.
Results may differ from a plain program's by a relative error of at most 0.0035.
The roundings to bfloat16 on the way count: a program that leaves them out, or rounds other values in their place, can miss the bound.
Values may be sent and summed in bfloat16 or wider, within the bound.
A program may use at most 64 MiB of HBM per device.

v0:
```python
import functools
import math

import jax
import jax.numpy as jnp
from jax import lax
from jax.experimental import pallas as pl
from jax.experimental.pallas import tpu as pltpu
from jax.sharding import PartitionSpec as P

MESH = pl.DeviceIdType.MESH
CONTRACT_LANES = (((1,), (1,)), ((), ()))


def dot(left, right):
    return jnp.dot(left, right, preferred_element_type=jnp.float32)


def swap_halves(tile):
    return pltpu.roll(tile, tile.shape[1] // 2, 1)


def exchange_kernel(
    n,
    slot,
    head_size,
    ids_ref,
    scale_ref,
    q_hbm,
    k_hbm,
    v_hbm,
    g_hbm,
    back_kq,
    back_v,
    q_ref,
    k_ref,
    v_ref,
    g_ref,
    send_place,
    send_qk,
    send_g,
    send_v,
    got_place,
    got_qk,
    got_g,
    got_v,
    region_qk,
    region_k,
    region_kt,
    region_g,
    region_v,
    bias,
    probs,
    probs_low,
    dscores,
    out_v,
    out_kq,
    ret_v,
    ret_kq,
    load_sem,
    send_sem,
    recv_sem,
):
    me = lax.axis_index("tile")
    tokens = q_ref.shape[0]
    capacity = n * slot
    width = 2 * head_size
    half = tokens // 2
    f32, bf16 = jnp.float32, jnp.bfloat16
    root = 1.0 / math.sqrt(head_size)

    barrier = pltpu.get_barrier_semaphore()
    for d in range(1, n):
        pl.semaphore_signal(
            barrier, inc=1, device_id={"tile": lax.rem(me + d, n)}, device_id_type=MESH
        )
    loads = [
        pltpu.make_async_copy(src, dst, load_sem.at[i])
        for i, (src, dst) in enumerate(
            ((q_hbm, q_ref), (k_hbm, k_ref), (g_hbm, g_ref), (v_hbm, v_ref))
        )
    ]
    for load in loads:
        load.start()

    def low_lanes(rows):
        return lax.broadcasted_iota(jnp.int32, (rows, width), 1) < head_size

    ids = ids_ref[...]
    mine = (lax.broadcasted_iota(jnp.int32, (n, tokens), 0) == ids).astype(f32)
    earlier = (
        lax.broadcasted_iota(jnp.int32, (tokens, tokens), 0)
        < lax.broadcasted_iota(jnp.int32, (tokens, tokens), 1)
    ).astype(bf16)
    rank = jnp.sum(dot(mine.astype(bf16), earlier) * mine, axis=0, keepdims=True)
    send_place[...] = jnp.broadcast_to(ids.astype(f32) * slot + rank, (8, tokens))

    low, low_half, low_cap = low_lanes(tokens), low_lanes(half), low_lanes(capacity)
    pairs = [
        (2 * pair, 2 * pair + 1, slice(pair * width, (pair + 1) * width))
        for pair in range(n // 2)
    ]
    loads[0].wait()
    loads[1].wait()
    for one, two, cols in pairs:
        lane_scale = jnp.where(low, scale_ref[one] * root, scale_ref[two] * root)
        q = (q_ref[:, cols].astype(f32) * lane_scale).astype(bf16).astype(f32)
        k = k_ref[:, cols].astype(f32)
        send_qk[one] = jnp.where(low, q, swap_halves(k)).astype(bf16)
        send_qk[two] = jnp.where(low, swap_halves(q), k).astype(bf16)

    pl.semaphore_wait(barrier, n - 1)

    def remote(kind, d, src, dst, peer):
        copy = pltpu.make_async_remote_copy(
            src_ref=src,
            dst_ref=dst,
            send_sem=send_sem.at[kind, d],
            recv_sem=recv_sem.at[kind, d],
            device_id={"tile": peer},
            device_id_type=MESH,
        )
        copy.start()
        return copy

    order = sorted(range(1, n), key=lambda d: -min(d, n - d))
    arrivals = [0] + order[::-1]
    place_copies, qk_copies, g_copies, v_copies = {}, {}, {}, {}
    for d in order:
        peer = lax.rem(me + d, n)
        place_copies[d] = remote(0, d, send_place, got_place.at[d], peer)
        qk_copies[d] = remote(1, d, send_qk.at[peer], got_qk.at[d], peer)

    def fold(ref, send, load):
        load.wait()
        for one, two, cols in pairs:
            top, bottom = ref[:half, cols].astype(f32), ref[half:, cols].astype(f32)
            send[one] = jnp.where(low_half, top, swap_halves(bottom)).astype(bf16)
            send[two] = jnp.where(low_half, swap_halves(top), bottom).astype(bf16)

    fold(g_ref, send_g, loads[2])
    fold(v_ref, send_v, loads[3])

    for d in order:
        peer = lax.rem(me + d, n)
        qk_copies[d].wait_send()
        g_copies[d] = remote(2, d, send_g.at[peer], got_g.at[d], peer)

    got_place[0] = send_place[...]

    def pick(d):
        rows = lax.broadcasted_iota(jnp.int32, (capacity, tokens), 0).astype(f32)
        return (rows == got_place[d][0:1, :]).astype(bf16)

    for d in arrivals:
        if d:
            place_copies[d].wait_recv()
            qk_copies[d].wait_recv()
        block = got_qk[d] if d else send_qk[me]
        placed = dot(pick(d), block)
        key_low = jnp.where(low_cap, swap_halves(placed), 0.0)
        region_qk[:, d] = placed.astype(bf16).reshape(n, slot, width)
        region_k[:, d] = key_low.astype(bf16).reshape(n, slot, width)

    counts = jnp.zeros((n, capacity), f32)
    table = jnp.zeros((8, tokens), f32)
    slot_of = lax.broadcasted_iota(jnp.int32, (n, capacity), 1)
    region_row = lax.broadcasted_iota(jnp.int32, (n, tokens), 0).astype(f32) * slot
    for d in range(n):
        place = got_place[d]
        held = (place[0:1, :] >= region_row) & (place[0:1, :] < region_row + slot)
        count = jnp.sum(held.astype(f32), axis=1, keepdims=True)
        here = (slot_of >= d * slot) & (slot_of < (d + 1) * slot)
        counts = jnp.where(here, count + d * slot, counts)
        table = jnp.where(lax.broadcasted_iota(jnp.int32, (8, tokens), 0) == d, place, table)
    bias_cols = jnp.transpose(jnp.where(slot_of.astype(f32) < counts, 0.0, -1e30))
    for r in range(n):
        bias[r] = jnp.broadcast_to(bias_cols[:, r : r + 1], (capacity, 128))
    place_cols = jnp.transpose(table)

    blocks = [slice(b * 128, (b + 1) * 128) for b in range(capacity // 128)]

    def score_step(r, carry):
        qk = region_qk[r].reshape(capacity, width)
        key_low = region_k[r].reshape(capacity, width)
        for b in blocks:
            scores = lax.dot_general(
                key_low, qk[b], CONTRACT_LANES, preferred_element_type=f32
            ) + bias[r]
            raw = jnp.exp(scores - jnp.max(scores, axis=0, keepdims=True))
            weights = raw * (1.0 / jnp.sum(raw, axis=0, keepdims=True))
            probs[r, :, b] = weights
            probs_low[r, :, b] = weights.astype(bf16)
        region_kt[r] = jnp.transpose(qk.astype(f32))[head_size:].astype(bf16)
        return carry

    lax.fori_loop(0, n, score_step, 0, unroll=n)

    for d in order:
        peer = lax.rem(me + d, n)
        g_copies[d].wait_send()
        v_copies[d] = remote(3, d, send_v.at[peer], got_v.at[d], peer)

    def unfold(got, send, d):
        folded = (got[d] if d else send[me]).astype(f32)
        return jnp.concatenate([folded, swap_halves(folded)], axis=0).astype(bf16)

    for d in arrivals:
        if d:
            g_copies[d].wait_recv()
        placed = dot(pick(d), unfold(got_g, send_g, d))
        region_g[:, d] = placed.astype(bf16).reshape(n, slot, width)

    def value_step(r, carry):
        grads = dot(probs_low[r], region_g[r].reshape(capacity, width))
        out_v[:, r] = grads.astype(bf16).reshape(n, slot, width)
        return carry

    lax.fori_loop(0, n, value_step, 0, unroll=n)

    def put(d, source):
        lanes = lax.broadcasted_iota(jnp.int32, (tokens, capacity), 1).astype(f32)
        rows = (lanes == place_cols[:, d : d + 1]).astype(bf16)
        return dot(rows, source[d].reshape(capacity, width))

    back_copies = []
    for d in order + [0]:
        grads = put(d, out_v)
        grads = jnp.where(low_half, grads[:half], swap_halves(grads[half:])).astype(bf16)
        if d:
            ret_v[d] = grads
            peer = lax.rem(me + n - d, n)
            back_copies.append(remote(4, d, ret_v.at[d], back_v.at[me], peer))
        else:
            back_v[me] = grads

    for d in arrivals:
        if d:
            v_copies[d].wait_recv()
        placed = jnp.where(low_cap, dot(pick(d), unfold(got_v, send_v, d)), 0.0)
        region_v[:, d] = placed.astype(bf16).reshape(n, slot, width)

    my_scale = scale_ref[me] * root

    def grad_step(r, carry):
        value_low = region_v[r].reshape(capacity, width)
        g = region_g[r].reshape(capacity, width)
        for b in blocks:
            dprobs = lax.dot_general(
                value_low, g[b], CONTRACT_LANES, preferred_element_type=f32
            )
            delta = jnp.sum(
                probs_low[r, :, b].astype(f32) * dprobs, axis=0, keepdims=True
            )
            dscores[r, :, b] = (probs[r, :, b] * (dprobs - delta)).astype(bf16)
        grads = dot(dscores[r], region_qk[r].reshape(capacity, width))
        raw_t = dot(region_kt[r], dscores[r]).astype(bf16).astype(f32) * my_scale
        raw = jnp.transpose(jnp.concatenate([raw_t, raw_t], axis=0))
        grads = jnp.where(low_cap, grads, raw)
        out_kq[:, r] = grads.astype(bf16).reshape(n, slot, width)
        return carry

    lax.fori_loop(0, n, grad_step, 0, unroll=n)

    for d in order + [0]:
        grads = put(d, out_kq).astype(bf16)
        if d:
            ret_kq[d] = grads
            peer = lax.rem(me + n - d, n)
            back_copies.append(remote(5, d, ret_kq.at[d], back_kq.at[me], peer))
        else:
            back_kq[me] = grads
    for copy in back_copies:
        copy.wait_recv()
    for copies in (place_copies, v_copies):
        for copy in copies.values():
            copy.wait_send()
    for copy in back_copies:
        copy.wait_send()


def unpack_kernel(n, kq_ref, v_ref, oq_ref, ok_ref, ov_ref):
    tokens, width = kq_ref.shape[1:]
    half = tokens // 2
    f32, bf16 = jnp.float32, jnp.bfloat16
    low = lax.broadcasted_iota(jnp.int32, (tokens, width), 1) < width // 2
    low_half = lax.broadcasted_iota(jnp.int32, (half, width), 1) < width // 2
    for pair in range(n // 2):
        cols = slice(pair * width, (pair + 1) * width)
        kq0, kq1 = kq_ref[2 * pair].astype(f32), kq_ref[2 * pair + 1].astype(f32)
        v0, v1 = v_ref[2 * pair].astype(f32), v_ref[2 * pair + 1].astype(f32)
        ok_ref[:, cols] = jnp.where(low, kq0, swap_halves(kq1)).astype(bf16)
        oq_ref[:, cols] = jnp.where(low, swap_halves(kq0), kq1).astype(bf16)
        ov_ref[:half, cols] = jnp.where(low_half, v0, swap_halves(v1)).astype(bf16)
        ov_ref[half:, cols] = jnp.where(low_half, swap_halves(v0), v1).astype(bf16)


def by_heads(queries, key_rows, value_rows, grad_out, owner_shard, logit_scale):
    n = lax.axis_size("tile")
    tokens, columns = queries.shape
    head_size = columns // n
    capacity = 2 * tokens
    slot = capacity // n
    width = 2 * head_size
    bf16, f32 = jnp.bfloat16, jnp.float32
    vmem = pl.BlockSpec(memory_space=pltpu.VMEM)
    smem = pl.BlockSpec(memory_space=pltpu.SMEM)
    anywhere = pl.BlockSpec(memory_space=pltpu.HBM)
    full = pltpu.VMEM((n, tokens, width), bf16)
    folded = pltpu.VMEM((n, tokens // 2, width), bf16)
    region = pltpu.VMEM((n, n, slot, width), bf16)
    square = (n, capacity, capacity)
    grant = 67043328 - 3 * n * tokens * width - 64 * 1024
    back_kq, back_v = pl.pallas_call(
        functools.partial(exchange_kernel, n, slot, head_size),
        out_shape=(
            pltpu.VMEM((n, tokens, width), bf16),
            pltpu.VMEM((n, tokens // 2, width), bf16),
        ),
        in_specs=[vmem, smem, anywhere, anywhere, anywhere, anywhere],
        out_specs=(vmem, vmem),
        scratch_shapes=[pltpu.VMEM((tokens, columns), bf16)] * 4
        + [pltpu.VMEM((8, tokens), f32), full, folded, folded]
        + [pltpu.VMEM((n, 8, tokens), f32), full, folded, folded]
        + [region, region, pltpu.VMEM((n, head_size, capacity), bf16), region, region]
        + [pltpu.VMEM((n, capacity, 128), f32), pltpu.VMEM(square, f32)]
        + [pltpu.VMEM(square, bf16), pltpu.VMEM(square, bf16)]
        + [region, region, folded, full]
        + [pltpu.SemaphoreType.DMA((4,))]
        + [pltpu.SemaphoreType.DMA((6, n))] * 2,
        compiler_params=pltpu.CompilerParams(
            collective_id=0, has_side_effects=True, vmem_limit_bytes=grant
        ),
    )(owner_shard.reshape(1, tokens), logit_scale, queries, key_rows, value_rows, grad_out)
    out = jax.ShapeDtypeStruct((tokens, columns), bf16)
    return pl.pallas_call(
        functools.partial(unpack_kernel, n),
        out_shape=(out, out, out),
        in_specs=[vmem, vmem],
        out_specs=(vmem, vmem, vmem),
        compiler_params=pltpu.CompilerParams(vmem_limit_bytes=8 * 1024 * 1024),
    )(back_kq, back_v)


def attend_heads(query_heads, key_heads, value_heads, dout_heads, live_rows):
    pair_mask = live_rows[None, :, None] & live_rows[None, None, :]
    scores = jnp.einsum("ihe,jhe->hij", query_heads, key_heads, preferred_element_type=jnp.float32)
    scores = jnp.where(pair_mask, scores, -1e30)
    row_max = jnp.max(scores, axis=2, keepdims=True)
    raw_weights = jnp.where(pair_mask, jnp.exp(scores - row_max), 0.0)
    row_sum = jnp.sum(raw_weights, axis=2, keepdims=True)
    row_sum = jnp.where(live_rows[None, :, None], row_sum, 1.0)
    weights = raw_weights / row_sum
    weights_low = weights.astype(jnp.bfloat16)
    attended = jnp.einsum(
        "hij,jhe->ihe", weights_low, value_heads, preferred_element_type=jnp.float32
    )
    row_delta = jnp.sum(dout_heads.astype(jnp.float32) * attended, axis=2)
    dprobs = jnp.einsum("ihe,jhe->hij", dout_heads, value_heads, preferred_element_type=jnp.float32)
    dscores = (weights * (dprobs - jnp.transpose(row_delta)[:, :, None])).astype(jnp.bfloat16)
    grad_value = jnp.einsum(
        "hij,ihe->jhe", weights_low, dout_heads, preferred_element_type=jnp.float32
    ).astype(jnp.bfloat16)
    grad_key = jnp.einsum(
        "hij,ihe->jhe", dscores, query_heads, preferred_element_type=jnp.float32
    ).astype(jnp.bfloat16)
    grad_raw = jnp.einsum(
        "hij,jhe->ihe", dscores, key_heads, preferred_element_type=jnp.float32
    ).astype(jnp.bfloat16)
    return (grad_raw, grad_key, grad_value)


def attend_items(query_items, key_items, value_items, dout_items, live_rows):
    capacity = query_items.shape[0]
    item_count = query_items.shape[1]
    head_size = query_items.shape[2] // 2
    outputs = ([], [], [])
    for item_index in range(item_count):
        halves = ([], [], [])
        for half_index in range(2):
            lower = half_index * head_size
            upper = lower + head_size
            pieces = attend_heads(
                query_items[:, item_index, lower:upper].reshape(capacity, 1, head_size),
                key_items[:, item_index, lower:upper].reshape(capacity, 1, head_size),
                value_items[:, item_index, lower:upper].reshape(capacity, 1, head_size),
                dout_items[:, item_index, lower:upper].reshape(capacity, 1, head_size),
                live_rows,
            )
            for holder, piece in zip(halves, pieces):
                holder.append(piece.reshape(capacity, head_size))
        for holder, parts_list in zip(outputs, halves):
            holder.append(jnp.concatenate(parts_list, axis=1))
    return tuple((jnp.stack(holder, axis=1) for holder in outputs))


def slot_places(owner_shard, shards, slot):
    one_hot = (owner_shard[:, None] == jnp.arange(shards, dtype=jnp.int32)[None, :]).astype(
        jnp.int32
    )
    before = jnp.cumsum(one_hot, axis=0) - one_hot
    rank = jnp.sum(before * one_hot, axis=1)
    return owner_shard * slot + rank


def by_regions(queries, key_rows, value_rows, grad_out, owner_shard, logit_scale):
    shards = lax.axis_size("tile")
    tok_rows, columns = queries.shape
    heads_here = logit_scale.shape[0]
    head_size = columns // heads_here
    capacity = 2 * tok_rows
    slot = capacity // shards
    pairs = heads_here // 2
    width = 2 * head_size
    slot_index = slot_places(owner_shard, shards, slot)
    scale_cols = jnp.repeat(logit_scale / math.sqrt(head_size), head_size)
    scaled = (queries.astype(jnp.float32) * scale_cols).astype(jnp.bfloat16)

    def spread(source):
        return jnp.zeros((capacity,) + source.shape[1:], source.dtype).at[slot_index].set(source)

    sent_query = spread(scaled)
    sent_key = spread(key_rows)
    sent_value = spread(value_rows)
    sent_dout = spread(grad_out)
    flags = spread(jnp.ones((tok_rows,), jnp.int32))
    got_query, got_key, got_value, got_dout, got_flags = (
        lax.all_to_all(sent_query, "tile", split_axis=0, concat_axis=0, tiled=True),
        lax.all_to_all(sent_key, "tile", split_axis=0, concat_axis=0, tiled=True),
        lax.all_to_all(sent_value, "tile", split_axis=0, concat_axis=0, tiled=True),
        lax.all_to_all(sent_dout, "tile", split_axis=0, concat_axis=0, tiled=True),
        lax.all_to_all(flags, "tile", split_axis=0, concat_axis=0, tiled=True),
    )
    grad_raw, grad_key, grad_value = attend_items(
        got_query.reshape(capacity, pairs, width),
        got_key.reshape(capacity, pairs, width),
        got_value.reshape(capacity, pairs, width),
        got_dout.reshape(capacity, pairs, width),
        got_flags > 0,
    )
    returned = (
        lax.all_to_all(
            grad_raw.reshape(capacity, columns), "tile", split_axis=0, concat_axis=0, tiled=True
        ),
        lax.all_to_all(
            grad_key.reshape(capacity, columns), "tile", split_axis=0, concat_axis=0, tiled=True
        ),
        lax.all_to_all(
            grad_value.reshape(capacity, columns), "tile", split_axis=0, concat_axis=0, tiled=True
        ),
    )
    grad_queries = (returned[0][slot_index].astype(jnp.float32) * scale_cols).astype(jnp.bfloat16)
    return (grad_queries, returned[1][slot_index], returned[2][slot_index])


def local(queries, key_rows, value_rows, grad_out, owner_shard, logit_scale):
    shards = lax.axis_size("tile")
    tokens, columns = queries.shape
    heads_here = logit_scale.shape[0]
    slot = 2 * tokens // shards
    fits = (
        shards == heads_here == 8
        and columns == heads_here * 64
        and slot % 16 == 0
        and (2 * tokens) % 128 == 0
        and tokens % 32 == 0
    )
    plan = by_heads if fits else by_regions
    return plan(queries, key_rows, value_rows, grad_out, owner_shard, logit_scale)


def solution(mesh):
    return jax.shard_map(
        local,
        mesh=mesh,
        in_specs=(
            P(("pages", "tile"), "mp"),
            P(("pages", "tile"), "mp"),
            P(("pages", "tile"), "mp"),
            P(("pages", "tile"), "mp"),
            P(("pages", "tile")),
            P("mp"),
        ),
        out_specs=(
            P(("pages", "tile"), "mp"),
            P(("pages", "tile"), "mp"),
            P(("pages", "tile"), "mp"),
        ),
        check_vma=False,
    )
```

profile of v0, /device:TPU:0, one launch (start us, length us, event | category | flops | bytes accessed | tf_op | source)
XLA Modules:
  0.0 45.6 jit_solution(7519635093723451362)
XLA Ops:
  0.6 43.9 %shard_map.85 = (bf16[8,192,128]{2,1,0:T(8,128)(2,1)S(1)}, bf16[8,96,128]{2,1,0:T(8,128)(2,1)S(1)}) custom-call(s32[1,192]{1,0:T(1,128)} %bitcast.1, f32[8]{0:T(128)} %scale_ref.1, bf16[192,512]{1,0:T(8,128)(2,1)} %q_hbm.1, bf16[192,512]{1,0:T(8,128)(2,1)} %k_hbm.1, bf16[192,512]{1,0:T(8,128)(2,1)} %v_hbm.1, bf16[192,512]{1,0:T(8,128)(2,1)} %g_hbm.1), custom_call_target="tpu_custom_call" | custom-call | tf_op jit(solution)/shard_map/pallas_call | solution.py:314
  44.5 1.0 %shard_map.86 = (bf16[192,512]{1,0:T(8,128)(2,1)}, bf16[192,512]{1,0:T(8,128)(2,1)}, bf16[192,512]{1,0:T(8,128)(2,1)}) custom-call(bf16[8,192,128]{2,1,0:T(8,128)(2,1)S(1)} %get-tuple-element.5.kq_ref, bf16[8,96,128]{2,1,0:T(8,128)(2,1)S(1)} %get-tuple-element.6.v_ref), custom_call_target="tpu_custom_call" | custom-call | tf_op jit(solution)/shard_map/pallas_call | solution.py:336
where the time goes:
time: 45.7 us; the launch traced here: 45.6 us
  Pallas kernels  44.9 us (98%)
  between operations  0.64 us (1%)
    pallas_call x1, Pallas kernels, by_heads(): pl.pallas_call(functools.partial(exchange_kernel, n, slot, head_size), ou...  43.9 us
    pallas_call x1, Pallas kernels, by_heads(): pl.pallas_call(functools.partial(unpack_kernel, n), out_shape=(out, out,...  1.04 us

commit v1 on v0

--- a/solution.py
+++ b/solution.py
@@ -24,14 +24,16 @@
     n,
     slot,
     head_size,
-    ids_ref,
-    scale_ref,
+    ids_hbm,
+    scale_hbm,
     q_hbm,
     k_hbm,
     v_hbm,
     g_hbm,
     back_kq,
     back_v,
+    ids_ref,
+    scale_ref,
     q_ref,
     k_ref,
     v_ref,
@@ -77,15 +79,23 @@
     loads = [
         pltpu.make_async_copy(src, dst, load_sem.at[i])
         for i, (src, dst) in enumerate(
-            ((q_hbm, q_ref), (k_hbm, k_ref), (g_hbm, g_ref), (v_hbm, v_ref))
+            (
+                (q_hbm, q_ref),
+                (k_hbm, k_ref),
+                (g_hbm, g_ref),
+                (v_hbm, v_ref),
+                (ids_hbm, ids_ref),
+                (scale_hbm, scale_ref),
+            )
         )
     ]
-    for load in loads:
-        load.start()
+    for i in (4, 5, 0, 1, 2, 3):
+        loads[i].start()
 
     def low_lanes(rows):
         return lax.broadcasted_iota(jnp.int32, (rows, width), 1) < head_size
 
+    loads[4].wait()
     ids = ids_ref[...]
     mine = (lax.broadcasted_iota(jnp.int32, (n, tokens), 0) == ids).astype(f32)
     earlier = (
@@ -93,13 +103,14 @@
         < lax.broadcasted_iota(jnp.int32, (tokens, tokens), 1)
     ).astype(bf16)
     rank = jnp.sum(dot(mine.astype(bf16), earlier) * mine, axis=0, keepdims=True)
-    send_place[...] = jnp.broadcast_to(ids.astype(f32) * slot + rank, (8, tokens))
+    send_place[...] = ids.astype(f32) * slot + rank
 
     low, low_half, low_cap = low_lanes(tokens), low_lanes(half), low_lanes(capacity)
     pairs = [
         (2 * pair, 2 * pair + 1, slice(pair * width, (pair + 1) * width))
         for pair in range(n // 2)
     ]
+    loads[5].wait()
     loads[0].wait()
     loads[1].wait()
     for one, two, cols in pairs:
@@ -124,11 +135,11 @@
         return copy
 
     order = sorted(range(1, n), key=lambda d: -min(d, n - d))
-    arrivals = [0] + order[::-1]
     place_copies, qk_copies, g_copies, v_copies = {}, {}, {}, {}
     for d in order:
+        place_copies[d] = remote(0, d, send_place, got_place.at[d], lax.rem(me + d, n))
+    for d in order:
         peer = lax.rem(me + d, n)
-        place_copies[d] = remote(0, d, send_place, got_place.at[d], peer)
         qk_copies[d] = remote(1, d, send_qk.at[peer], got_qk.at[d], peer)
 
     def fold(ref, send, load):
@@ -139,36 +150,25 @@
             send[two] = jnp.where(low_half, swap_halves(top), bottom).astype(bf16)
 
     fold(g_ref, send_g, loads[2])
+    for d in order:
+        peer = lax.rem(me + d, n)
+        g_copies[d] = remote(2, d, send_g.at[peer], got_g.at[d], peer)
     fold(v_ref, send_v, loads[3])
-
     for d in order:
         peer = lax.rem(me + d, n)
-        qk_copies[d].wait_send()
-        g_copies[d] = remote(2, d, send_g.at[peer], got_g.at[d], peer)
+        v_copies[d] = remote(3, d, send_v.at[peer], got_v.at[d], peer)
 
     got_place[0] = send_place[...]
-
-    def pick(d):
-        rows = lax.broadcasted_iota(jnp.int32, (capacity, tokens), 0).astype(f32)
-        return (rows == got_place[d][0:1, :]).astype(bf16)
-
-    for d in arrivals:
-        if d:
-            place_copies[d].wait_recv()
-            qk_copies[d].wait_recv()
-        block = got_qk[d] if d else send_qk[me]
-        placed = dot(pick(d), block)
-        key_low = jnp.where(low_cap, swap_halves(placed), 0.0)
-        region_qk[:, d] = placed.astype(bf16).reshape(n, slot, width)
-        region_k[:, d] = key_low.astype(bf16).reshape(n, slot, width)
+    for d in order:
+        place_copies[d].wait_recv()
 
     counts = jnp.zeros((n, capacity), f32)
     table = jnp.zeros((8, tokens), f32)
     slot_of = lax.broadcasted_iota(jnp.int32, (n, capacity), 1)
     region_row = lax.broadcasted_iota(jnp.int32, (n, tokens), 0).astype(f32) * slot
     for d in range(n):
-        place = got_place[d]
-        held = (place[0:1, :] >= region_row) & (place[0:1, :] < region_row + slot)
+        place = jnp.broadcast_to(got_place[d], (8, tokens))
+        held = (place >= region_row) & (place < region_row + slot)
         count = jnp.sum(held.astype(f32), axis=1, keepdims=True)
         here = (slot_of >= d * slot) & (slot_of < (d + 1) * slot)
         counts = jnp.where(here, count + d * slot, counts)
@@ -177,6 +177,19 @@
     for r in range(n):
         bias[r] = jnp.broadcast_to(bias_cols[:, r : r + 1], (capacity, 128))
     place_cols = jnp.transpose(table)
+
+    def pick(d):
+        rows = lax.broadcasted_iota(jnp.int32, (capacity, tokens), 0).astype(f32)
+        return (rows == got_place[d]).astype(bf16)
+
+    for d in order:
+        qk_copies[d].wait_recv()
+    for d in range(n):
+        block = got_qk[d] if d else send_qk[me]
+        placed = dot(pick(d), block)
+        key_low = jnp.where(low_cap, swap_halves(placed), 0.0)
+        region_qk[:, d] = placed.astype(bf16).reshape(n, slot, width)
+        region_k[:, d] = key_low.astype(bf16).reshape(n, slot, width)
 
     blocks = [slice(b * 128, (b + 1) * 128) for b in range(capacity // 128)]
 
@@ -196,18 +209,13 @@
 
     lax.fori_loop(0, n, score_step, 0, unroll=n)
 
-    for d in order:
-        peer = lax.rem(me + d, n)
-        g_copies[d].wait_send()
-        v_copies[d] = remote(3, d, send_v.at[peer], got_v.at[d], peer)
-
     def unfold(got, send, d):
         folded = (got[d] if d else send[me]).astype(f32)
         return jnp.concatenate([folded, swap_halves(folded)], axis=0).astype(bf16)
 
-    for d in arrivals:
-        if d:
-            g_copies[d].wait_recv()
+    for d in order:
+        g_copies[d].wait_recv()
+    for d in range(n):
         placed = dot(pick(d), unfold(got_g, send_g, d))
         region_g[:, d] = placed.astype(bf16).reshape(n, slot, width)
 
@@ -223,20 +231,24 @@
         rows = (lanes == place_cols[:, d : d + 1]).astype(bf16)
         return dot(rows, source[d].reshape(capacity, width))
 
+    batches = (order[: n // 2], order[n // 2 :] + [0])
     back_copies = []
-    for d in order + [0]:
-        grads = put(d, out_v)
-        grads = jnp.where(low_half, grads[:half], swap_halves(grads[half:])).astype(bf16)
-        if d:
-            ret_v[d] = grads
-            peer = lax.rem(me + n - d, n)
-            back_copies.append(remote(4, d, ret_v.at[d], back_v.at[me], peer))
-        else:
-            back_v[me] = grads
-
-    for d in arrivals:
-        if d:
-            v_copies[d].wait_recv()
+    for batch in batches:
+        for d in batch:
+            grads = put(d, out_v)
+            grads = jnp.where(low_half, grads[:half], swap_halves(grads[half:])).astype(bf16)
+            if d:
+                ret_v[d] = grads
+            else:
+                back_v[me] = grads
+        for d in batch:
+            if d:
+                peer = lax.rem(me + n - d, n)
+                back_copies.append(remote(4, d, ret_v.at[d], back_v.at[me], peer))
+
+    for d in order:
+        v_copies[d].wait_recv()
+    for d in range(n):
         placed = jnp.where(low_cap, dot(pick(d), unfold(got_v, send_v, d)), 0.0)
         region_v[:, d] = placed.astype(bf16).reshape(n, slot, width)
 
@@ -262,17 +274,20 @@
 
     lax.fori_loop(0, n, grad_step, 0, unroll=n)
 
-    for d in order + [0]:
-        grads = put(d, out_kq).astype(bf16)
-        if d:
-            ret_kq[d] = grads
-            peer = lax.rem(me + n - d, n)
-            back_copies.append(remote(5, d, ret_kq.at[d], back_kq.at[me], peer))
-        else:
-            back_kq[me] = grads
+    for batch in batches:
+        for d in batch:
+            grads = put(d, out_kq).astype(bf16)
+            if d:
+                ret_kq[d] = grads
+            else:
+                back_kq[me] = grads
+        for d in batch:
+            if d:
+                peer = lax.rem(me + n - d, n)
+                back_copies.append(remote(5, d, ret_kq.at[d], back_kq.at[me], peer))
     for copy in back_copies:
         copy.wait_recv()
-    for copies in (place_copies, v_copies):
+    for copies in (place_copies, qk_copies, g_copies, v_copies):
         for copy in copies.values():
             copy.wait_send()
     for copy in back_copies:
@@ -304,7 +319,6 @@
     width = 2 * head_size
     bf16, f32 = jnp.bfloat16, jnp.float32
     vmem = pl.BlockSpec(memory_space=pltpu.VMEM)
-    smem = pl.BlockSpec(memory_space=pltpu.SMEM)
     anywhere = pl.BlockSpec(memory_space=pltpu.HBM)
     full = pltpu.VMEM((n, tokens, width), bf16)
     folded = pltpu.VMEM((n, tokens // 2, width), bf16)
@@ -317,16 +331,17 @@
             pltpu.VMEM((n, tokens, width), bf16),
             pltpu.VMEM((n, tokens // 2, width), bf16),
         ),
-        in_specs=[vmem, smem, anywhere, anywhere, anywhere, anywhere],
+        in_specs=[anywhere] * 6,
         out_specs=(vmem, vmem),
-        scratch_shapes=[pltpu.VMEM((tokens, columns), bf16)] * 4
-        + [pltpu.VMEM((8, tokens), f32), full, folded, folded]
-        + [pltpu.VMEM((n, 8, tokens), f32), full, folded, folded]
+        scratch_shapes=[pltpu.VMEM((1, tokens), jnp.int32), pltpu.SMEM((n,), f32)]
+        + [pltpu.VMEM((tokens, columns), bf16)] * 4
+        + [pltpu.VMEM((1, tokens), f32), full, folded, folded]
+        + [pltpu.VMEM((n, 1, tokens), f32), full, folded, folded]
         + [region, region, pltpu.VMEM((n, head_size, capacity), bf16), region, region]
         + [pltpu.VMEM((n, capacity, 128), f32), pltpu.VMEM(square, f32)]
         + [pltpu.VMEM(square, bf16), pltpu.VMEM(square, bf16)]
         + [region, region, folded, full]
-        + [pltpu.SemaphoreType.DMA((4,))]
+        + [pltpu.SemaphoreType.DMA((6,))]
         + [pltpu.SemaphoreType.DMA((6, n))] * 2,
         compiler_params=pltpu.CompilerParams(
             collective_id=0, has_side_effects=True, vmem_limit_bytes=grant

time: 45.7 us -> 41 us (0.90)
  Pallas kernels: 44.9 us -> 40.2 us
    pallas_call x1, Pallas kernels: 43.9 us -> 39.1 us  [by_heads(): pl.pallas_call(functools.partial(exchange_kernel, n, slot, head_size), ou...]
where the time goes in v1:
time: 41 us; the launch traced here: 40.8 us
  Pallas kernels  40.2 us (98%)
  between operations  0.64 us (2%)
    pallas_call x1, Pallas kernels, by_heads(): pl.pallas_call(functools.partial(exchange_kernel, n, slot, head_size), ou...  39.1 us
    pallas_call x1, Pallas kernels, by_heads(): pl.pallas_call(functools.partial(unpack_kernel, n), out_shape=(out, out,...  1.04 us

profile of v1, /device:TPU:0, one launch (start us, length us, event | category | flops | bytes accessed | tf_op | source)
XLA Modules:
  0.0 40.8 jit_solution(7816012074348255672)
XLA Ops:
  0.6 39.1 %shard_map.85 = (bf16[8,192,128]{2,1,0:T(8,128)(2,1)S(1)}, bf16[8,96,128]{2,1,0:T(8,128)(2,1)S(1)}) custom-call(s32[1,192]{1,0:T(1,128)} %bitcast.1, f32[8]{0:T(128)} %scale_hbm.1, bf16[192,512]{1,0:T(8,128)(2,1)} %q_hbm.1, bf16[192,512]{1,0:T(8,128)(2,1)} %k_hbm.1, bf16[192,512]{1,0:T(8,128)(2,1)} %v_hbm.1, bf16[192,512]{1,0:T(8,128)(2,1)} %g_hbm.1), custom_call_target="tpu_custom_call" | custom-call | tf_op jit(solution)/shard_map/pallas_call | solution.py:328
  39.8 1.0 %shard_map.86 = (bf16[192,512]{1,0:T(8,128)(2,1)}, bf16[192,512]{1,0:T(8,128)(2,1)}, bf16[192,512]{1,0:T(8,128)(2,1)}) custom-call(bf16[8,192,128]{2,1,0:T(8,128)(2,1)S(1)} %get-tuple-element.5.kq_ref, bf16[8,96,128]{2,1,0:T(8,128)(2,1)S(1)} %get-tuple-element.6.v_ref), custom_call_target="tpu_custom_call" | custom-call | tf_op jit(solution)/shard_map/pallas_call | solution.py:351

commit v2 on v1

--- a/solution.py
+++ b/solution.py
@@ -34,10 +34,7 @@
     back_v,
     ids_ref,
     scale_ref,
-    q_ref,
-    k_ref,
-    v_ref,
-    g_ref,
+    rows_ref,
     send_place,
     send_qk,
     send_g,
@@ -46,9 +43,9 @@
     got_qk,
     got_g,
     got_v,
+    region_q,
     region_qk,
     region_k,
-    region_kt,
     region_g,
     region_v,
     bias,
@@ -64,7 +61,7 @@
     recv_sem,
 ):
     me = lax.axis_index("tile")
-    tokens = q_ref.shape[0]
+    tokens = send_place.shape[1]
     capacity = n * slot
     width = 2 * head_size
     half = tokens // 2
@@ -80,22 +77,68 @@
         pltpu.make_async_copy(src, dst, load_sem.at[i])
         for i, (src, dst) in enumerate(
             (
-                (q_hbm, q_ref),
-                (k_hbm, k_ref),
-                (g_hbm, g_ref),
-                (v_hbm, v_ref),
                 (ids_hbm, ids_ref),
+                (q_hbm, rows_ref.at[0]),
+                (k_hbm, rows_ref.at[1]),
                 (scale_hbm, scale_ref),
+                (g_hbm, rows_ref.at[2]),
+                (v_hbm, rows_ref.at[3]),
             )
         )
     ]
-    for i in (4, 5, 0, 1, 2, 3):
-        loads[i].start()
+    for load in loads:
+        load.start()
+
+    def wait_bytes(refs, sem):
+        pltpu.make_async_copy(refs, refs, sem).wait()
+
+    bits = [me % 2, me // 2 % 2, me // 4]
+
+    def across(d):
+        flips = [d % 2, d // 2 % 2, d // 4]
+        return sum((1 - b if f else b) * 2**i for i, (b, f) in enumerate(zip(bits, flips)))
+
+    inner = (bits[1] + bits[2]) % 2
+    early, late = (4, 5), (6, 7, 2, 3, 1)
+    steps = list(zip((4, 5, 6, 7, 2, 3, 1), (2, 3, 1, 4, 5, 6, 7)))
+
+    def pick_step(outside, inside):
+        return outside + inner * (inside - outside)
+
+    def remote(src, dst, send, recv, peer):
+        pltpu.make_async_remote_copy(
+            src_ref=src,
+            dst_ref=dst,
+            send_sem=send_sem.at[send],
+            recv_sem=recv_sem.at[recv],
+            device_id={"tile": peer},
+            device_id_type=MESH,
+        ).start()
+
+    def scatter(send, got, kind, groups):
+        for a, b in steps:
+            d = pick_step(a, b)
+            peer = pick_step(across(a), across(b))
+            group = pick_step(groups[a in early], groups[b in early])
+            remote(send.at[peer], got.at[d], kind, group, peer)
 
     def low_lanes(rows):
         return lax.broadcasted_iota(jnp.int32, (rows, width), 1) < head_size
 
-    loads[4].wait()
+    low, low_half, low_cap = low_lanes(tokens), low_lanes(half), low_lanes(capacity)
+    pairs = [
+        (2 * pair, 2 * pair + 1, slice(pair * width, (pair + 1) * width))
+        for pair in range(n // 2)
+    ]
+    for load in loads[:4]:
+        load.wait()
+    for one, two, cols in pairs:
+        lane_scale = jnp.where(low, scale_ref[one] * root, scale_ref[two] * root)
+        q = (rows_ref[0, :, cols].astype(f32) * lane_scale).astype(bf16).astype(f32)
+        k = rows_ref[1, :, cols].astype(f32)
+        send_qk[one] = jnp.where(low, q, swap_halves(k)).astype(bf16)
+        send_qk[two] = jnp.where(low, swap_halves(q), k).astype(bf16)
+
     ids = ids_ref[...]
     mine = (lax.broadcasted_iota(jnp.int32, (n, tokens), 0) == ids).astype(f32)
     earlier = (
@@ -103,118 +146,98 @@
         < lax.broadcasted_iota(jnp.int32, (tokens, tokens), 1)
     ).astype(bf16)
     rank = jnp.sum(dot(mine.astype(bf16), earlier) * mine, axis=0, keepdims=True)
-    send_place[...] = ids.astype(f32) * slot + rank
-
-    low, low_half, low_cap = low_lanes(tokens), low_lanes(half), low_lanes(capacity)
-    pairs = [
-        (2 * pair, 2 * pair + 1, slice(pair * width, (pair + 1) * width))
-        for pair in range(n // 2)
-    ]
-    loads[5].wait()
-    loads[0].wait()
-    loads[1].wait()
-    for one, two, cols in pairs:
-        lane_scale = jnp.where(low, scale_ref[one] * root, scale_ref[two] * root)
-        q = (q_ref[:, cols].astype(f32) * lane_scale).astype(bf16).astype(f32)
-        k = k_ref[:, cols].astype(f32)
-        send_qk[one] = jnp.where(low, q, swap_halves(k)).astype(bf16)
-        send_qk[two] = jnp.where(low, swap_halves(q), k).astype(bf16)
+    places = ids.astype(f32) * slot + rank
+    send_place[...] = places
 
     pl.semaphore_wait(barrier, n - 1)
 
-    def remote(kind, d, src, dst, peer):
-        copy = pltpu.make_async_remote_copy(
-            src_ref=src,
-            dst_ref=dst,
-            send_sem=send_sem.at[kind, d],
-            recv_sem=recv_sem.at[kind, d],
-            device_id={"tile": peer},
-            device_id_type=MESH,
-        )
-        copy.start()
-        return copy
-
-    order = sorted(range(1, n), key=lambda d: -min(d, n - d))
-    place_copies, qk_copies, g_copies, v_copies = {}, {}, {}, {}
-    for d in order:
-        place_copies[d] = remote(0, d, send_place, got_place.at[d], lax.rem(me + d, n))
-    for d in order:
-        peer = lax.rem(me + d, n)
-        qk_copies[d] = remote(1, d, send_qk.at[peer], got_qk.at[d], peer)
-
-    def fold(ref, send, load):
-        load.wait()
+    for d in range(1, n):
+        remote(send_place, got_place.at[d], 0, 0, across(d))
+    scatter(send_qk, got_qk, 1, (2, 1))
+    got_place[0] = places
+
+    def fold(index, send):
         for one, two, cols in pairs:
-            top, bottom = ref[:half, cols].astype(f32), ref[half:, cols].astype(f32)
+            top = rows_ref[index, :half, cols].astype(f32)
+            bottom = rows_ref[index, half:, cols].astype(f32)
             send[one] = jnp.where(low_half, top, swap_halves(bottom)).astype(bf16)
             send[two] = jnp.where(low_half, swap_halves(top), bottom).astype(bf16)
 
-    fold(g_ref, send_g, loads[2])
-    for d in order:
-        peer = lax.rem(me + d, n)
-        g_copies[d] = remote(2, d, send_g.at[peer], got_g.at[d], peer)
-    fold(v_ref, send_v, loads[3])
-    for d in order:
-        peer = lax.rem(me + d, n)
-        v_copies[d] = remote(3, d, send_v.at[peer], got_v.at[d], peer)
-
-    got_place[0] = send_place[...]
-    for d in order:
-        place_copies[d].wait_recv()
-
-    counts = jnp.zeros((n, capacity), f32)
-    table = jnp.zeros((8, tokens), f32)
+    loads[4].wait()
+    loads[5].wait()
+    fold(2, send_g)
+    fold(3, send_v)
+
+    wait_bytes(got_place.at[1:], recv_sem.at[0])
+    wait_bytes(got_qk.at[: len(early)], recv_sem.at[1])
+    scatter(send_g, got_g, 2, (4, 3))
+
+    lane_of = lax.broadcasted_iota(jnp.int32, (capacity, width), 1)
     slot_of = lax.broadcasted_iota(jnp.int32, (n, capacity), 1)
+    row_of = lax.broadcasted_iota(jnp.int32, (n, capacity), 0)
     region_row = lax.broadcasted_iota(jnp.int32, (n, tokens), 0).astype(f32) * slot
+    first_slot = row_of.astype(f32) * slot
+    filled = jnp.zeros((n, capacity), f32)
+    table = jnp.zeros((n, tokens), f32)
     for d in range(n):
-        place = jnp.broadcast_to(got_place[d], (8, tokens))
+        place = jnp.broadcast_to(got_place[d], (n, tokens))
         held = (place >= region_row) & (place < region_row + slot)
-        count = jnp.sum(held.astype(f32), axis=1, keepdims=True)
-        here = (slot_of >= d * slot) & (slot_of < (d + 1) * slot)
-        counts = jnp.where(here, count + d * slot, counts)
-        table = jnp.where(lax.broadcasted_iota(jnp.int32, (8, tokens), 0) == d, place, table)
-    bias_cols = jnp.transpose(jnp.where(slot_of.astype(f32) < counts, 0.0, -1e30))
-    for r in range(n):
-        bias[r] = jnp.broadcast_to(bias_cols[:, r : r + 1], (capacity, 128))
+        end = jnp.sum(held.astype(f32), axis=1, keepdims=True) + first_slot
+        used = (slot_of.astype(f32) < end) & (slot_of.astype(f32) >= first_slot)
+        used = jnp.sum(used.astype(f32), axis=0, keepdims=True)
+        filled = jnp.where(row_of == d, used, filled)
+        table = jnp.where(lax.broadcasted_iota(jnp.int32, (n, tokens), 0) == d, place, table)
+    bias_cols = jnp.transpose((filled - 1.0) * 1e30)
+    for d in range(n):
+        bias[d] = jnp.where(lane_of == head_size, bias_cols[:, d : d + 1], 0.0)
     place_cols = jnp.transpose(table)
 
     def pick(d):
         rows = lax.broadcasted_iota(jnp.int32, (capacity, tokens), 0).astype(f32)
         return (rows == got_place[d]).astype(bf16)
 
-    for d in order:
-        qk_copies[d].wait_recv()
-    for d in range(n):
-        block = got_qk[d] if d else send_qk[me]
-        placed = dot(pick(d), block)
-        key_low = jnp.where(low_cap, swap_halves(placed), 0.0)
+    mark_one = (lane_of == head_size).astype(f32)
+
+    def place_qk(d):
+        placed = dot(pick(d), got_qk[d] if d else send_qk[me])
+        key_low = jnp.where(low_cap, swap_halves(placed), bias[d])
+        query = jnp.where(low_cap, placed, mark_one)
         region_qk[:, d] = placed.astype(bf16).reshape(n, slot, width)
         region_k[:, d] = key_low.astype(bf16).reshape(n, slot, width)
-
-    blocks = [slice(b * 128, (b + 1) * 128) for b in range(capacity // 128)]
-
-    def score_step(r, carry):
-        qk = region_qk[r].reshape(capacity, width)
-        key_low = region_k[r].reshape(capacity, width)
-        for b in blocks:
-            scores = lax.dot_general(
-                key_low, qk[b], CONTRACT_LANES, preferred_element_type=f32
-            ) + bias[r]
-            raw = jnp.exp(scores - jnp.max(scores, axis=0, keepdims=True))
-            weights = raw * (1.0 / jnp.sum(raw, axis=0, keepdims=True))
-            probs[r, :, b] = weights
-            probs_low[r, :, b] = weights.astype(bf16)
-        region_kt[r] = jnp.transpose(qk.astype(f32))[head_size:].astype(bf16)
+        region_q[:, d * slot : (d + 1) * slot] = query.astype(bf16).reshape(n, slot, width)
+
+    for d in (0,) + early:
+        place_qk(d)
+    wait_bytes(got_qk.at[: len(late)], recv_sem.at[2])
+    for d in late:
+        place_qk(d)
+
+    nb = capacity // 128
+    blocks = [slice(b * 128, (b + 1) * 128) for b in range(nb)]
+
+    def score_step(t, carry):
+        r, b = t // nb, pl.multiple_of(t % nb * 128, 128)
+        scores = lax.dot_general(
+            region_k[r].reshape(capacity, width),
+            region_q[r, pl.ds(b, 128)],
+            CONTRACT_LANES,
+            preferred_element_type=f32,
+        )
+        raw = jnp.exp(scores - jnp.max(scores, axis=0, keepdims=True))
+        weights = raw * (1.0 / jnp.sum(raw, axis=0, keepdims=True))
+        probs[r, :, pl.ds(b, 128)] = weights
+        probs_low[r, :, pl.ds(b, 128)] = weights.astype(bf16)
         return carry
 
-    lax.fori_loop(0, n, score_step, 0, unroll=n)
+    scatter(send_v, got_v, 3, (5, 5))
+    lax.fori_loop(0, n * nb, score_step, 0, unroll=n * nb)
 
     def unfold(got, send, d):
         folded = (got[d] if d else send[me]).astype(f32)
         return jnp.concatenate([folded, swap_halves(folded)], axis=0).astype(bf16)
 
-    for d in order:
-        g_copies[d].wait_recv()
+    wait_bytes(got_g.at[: len(early)], recv_sem.at[3])
+    wait_bytes(got_g.at[: len(late)], recv_sem.at[4])
     for d in range(n):
         placed = dot(pick(d), unfold(got_g, send_g, d))
         region_g[:, d] = placed.astype(bf16).reshape(n, slot, width)
@@ -231,23 +254,39 @@
         rows = (lanes == place_cols[:, d : d + 1]).astype(bf16)
         return dot(rows, source[d].reshape(capacity, width))
 
-    batches = (order[: n // 2], order[n // 2 :] + [0])
-    back_copies = []
-    for batch in batches:
-        for d in batch:
-            grads = put(d, out_v)
-            grads = jnp.where(low_half, grads[:half], swap_halves(grads[half:])).astype(bf16)
-            if d:
-                ret_v[d] = grads
-            else:
-                back_v[me] = grads
-        for d in batch:
-            if d:
-                peer = lax.rem(me + n - d, n)
-                back_copies.append(remote(4, d, ret_v.at[d], back_v.at[me], peer))
-
-    for d in order:
-        v_copies[d].wait_recv()
+    quad = n // 2
+    mine_low = me % quad
+
+    def low_xor(a):
+        return (a + mine_low) % 2 + (a // 2 + mine_low // 2) % 2 * 2
+
+    far_slots = [quad + low_xor(k) for k in range(quad)]
+    far_peers = [k + quad * (1 - bits[2]) for k in range(quad)]
+    near = [s + (s - mine_low + quad) // quad for s in range(quad - 1)]
+    near_slots = [low_xor(k) for k in near]
+    near_peers = [k + quad * bits[2] for k in near]
+
+    def give_back(ret, back, kind, make):
+        for slots, peers, made in (
+            (far_slots, far_peers, range(quad, n)),
+            (near_slots, near_peers, range(quad)),
+        ):
+            for d in made:
+                grads = make(d)
+                if d:
+                    ret[d] = grads
+                else:
+                    back[me] = grads
+            for d, peer in zip(slots, peers):
+                remote(ret.at[d], back.at[me], kind, kind + 2, peer)
+
+    def value_back(d):
+        grads = put(d, out_v)
+        return jnp.where(low_half, grads[:half], swap_halves(grads[half:])).astype(bf16)
+
+    give_back(ret_v, back_v, 4, value_back)
+
+    wait_bytes(got_v.at[1:], recv_sem.at[5])
     for d in range(n):
         placed = jnp.where(low_cap, dot(pick(d), unfold(got_v, send_v, d)), 0.0)
         region_v[:, d] = placed.astype(bf16).reshape(n, slot, width)
@@ -257,16 +296,19 @@
     def grad_step(r, carry):
         value_low = region_v[r].reshape(capacity, width)
         g = region_g[r].reshape(capacity, width)
+        qk = region_qk[r].reshape(capacity, width)
+        value_t = jnp.transpose(value_low.astype(f32))[:head_size].astype(bf16)
+        g_t = jnp.transpose(g.astype(f32))[:head_size]
+        key_t = jnp.transpose(qk.astype(f32))[head_size:].astype(bf16)
+        attended = dot(value_t, probs_low[r])
+        delta = jnp.sum(g_t * attended, axis=0, keepdims=True)
         for b in blocks:
             dprobs = lax.dot_general(
                 value_low, g[b], CONTRACT_LANES, preferred_element_type=f32
             )
-            delta = jnp.sum(
-                probs_low[r, :, b].astype(f32) * dprobs, axis=0, keepdims=True
-            )
-            dscores[r, :, b] = (probs[r, :, b] * (dprobs - delta)).astype(bf16)
-        grads = dot(dscores[r], region_qk[r].reshape(capacity, width))
-        raw_t = dot(region_kt[r], dscores[r]).astype(bf16).astype(f32) * my_scale
+            dscores[r, :, b] = (probs[r, :, b] * (dprobs - delta[:, b])).astype(bf16)
+        grads = dot(dscores[r], qk)
+        raw_t = dot(key_t, dscores[r]).astype(bf16).astype(f32) * my_scale
         raw = jnp.transpose(jnp.concatenate([raw_t, raw_t], axis=0))
         grads = jnp.where(low_cap, grads, raw)
         out_kq[:, r] = grads.astype(bf16).reshape(n, slot, width)
@@ -274,24 +316,12 @@
 
     lax.fori_loop(0, n, grad_step, 0, unroll=n)
 
-    for batch in batches:
-        for d in batch:
-            grads = put(d, out_kq).astype(bf16)
-            if d:
-                ret_kq[d] = grads
-            else:
-                back_kq[me] = grads
-        for d in batch:
-            if d:
-                peer = lax.rem(me + n - d, n)
-                back_copies.append(remote(5, d, ret_kq.at[d], back_kq.at[me], peer))
-    for copy in back_copies:
-        copy.wait_recv()
-    for copies in (place_copies, qk_copies, g_copies, v_copies):
-        for copy in copies.values():
-            copy.wait_send()
-    for copy in back_copies:
-        copy.wait_send()
+    give_back(ret_kq, back_kq, 5, lambda d: put(d, out_kq).astype(bf16))
+
+    wait_bytes(back_v.at[1:], recv_sem.at[6])
+    wait_bytes(back_kq.at[1:], recv_sem.at[7])
+    for kind, refs in enumerate((got_place, send_qk, send_g, send_v, ret_v, ret_kq)):
+        wait_bytes(refs.at[1:], send_sem.at[kind])
 
 
 def unpack_kernel(n, kq_ref, v_ref, oq_ref, ok_ref, ov_ref):
@@ -334,15 +364,15 @@
         in_specs=[anywhere] * 6,
         out_specs=(vmem, vmem),
         scratch_shapes=[pltpu.VMEM((1, tokens), jnp.int32), pltpu.SMEM((n,), f32)]
-        + [pltpu.VMEM((tokens, columns), bf16)] * 4
+        + [pltpu.VMEM((4, tokens, columns), bf16)]
         + [pltpu.VMEM((1, tokens), f32), full, folded, folded]
         + [pltpu.VMEM((n, 1, tokens), f32), full, folded, folded]
-        + [region, region, pltpu.VMEM((n, head_size, capacity), bf16), region, region]
+        + [pltpu.VMEM((n, capacity, width), bf16), region, region, region, region]
         + [pltpu.VMEM((n, capacity, 128), f32), pltpu.VMEM(square, f32)]
         + [pltpu.VMEM(square, bf16), pltpu.VMEM(square, bf16)]
         + [region, region, folded, full]
-        + [pltpu.SemaphoreType.DMA((6,))]
-        + [pltpu.SemaphoreType.DMA((6, n))] * 2,
+        + [pltpu.SemaphoreType.DMA((6,))] * 2
+        + [pltpu.SemaphoreType.DMA((8,))],
         compiler_params=pltpu.CompilerParams(
             collective_id=0, has_side_effects=True, vmem_limit_bytes=grant
         ),

time: 41 us -> 38.8 us (0.946)
  Pallas kernels: 40.2 us -> 38 us
    pallas_call x1, Pallas kernels: 39.1 us -> 37 us  [by_heads(): pl.pallas_call(functools.partial(exchange_kernel, n, slot, head_size), ou...]
where the time goes in v2:
time: 38.8 us; the launch traced here: 38.7 us
  Pallas kernels  38 us (98%)
  between operations  0.64 us (2%)
    pallas_call x1, Pallas kernels, by_heads(): pl.pallas_call(functools.partial(exchange_kernel, n, slot, head_size), ou...  37 us
    pallas_call x1, Pallas kernels, by_heads(): pl.pallas_call(functools.partial(unpack_kernel, n), out_shape=(out, out,...  1.04 us

profile of v2, /device:TPU:0, one launch (start us, length us, event | category | flops | bytes accessed | tf_op | source)
XLA Modules:
  0.0 38.7 jit_solution(7911740706865525625)
XLA Ops:
  0.6 37.0 %shard_map.85 = (bf16[8,192,128]{2,1,0:T(8,128)(2,1)S(1)}, bf16[8,96,128]{2,1,0:T(8,128)(2,1)S(1)}) custom-call(s32[1,192]{1,0:T(1,128)} %bitcast.1, f32[8]{0:T(128)} %scale_hbm.1, bf16[192,512]{1,0:T(8,128)(2,1)} %q_hbm.1, bf16[192,512]{1,0:T(8,128)(2,1)} %k_hbm.1, bf16[192,512]{1,0:T(8,128)(2,1)} %v_hbm.1, bf16[192,512]{1,0:T(8,128)(2,1)} %g_hbm.1), custom_call_target="tpu_custom_call" | custom-call | tf_op jit(solution)/shard_map/pallas_call | solution.py:358
  37.6 1.0 %shard_map.86 = (bf16[192,512]{1,0:T(8,128)(2,1)}, bf16[192,512]{1,0:T(8,128)(2,1)}, bf16[192,512]{1,0:T(8,128)(2,1)}) custom-call(bf16[8,192,128]{2,1,0:T(8,128)(2,1)S(1)} %get-tuple-element.5.kq_ref, bf16[8,96,128]{2,1,0:T(8,128)(2,1)S(1)} %get-tuple-element.6.v_ref), custom_call_target="tpu_custom_call" | custom-call | tf_op jit(solution)/shard_map/pallas_call | solution.py:381
